TPU v7x, 512 devices: a whole 4x8x8 slice. The times are simulated.
512 devices in a mesh: lat: 128 (over z, y, core), tok: 4 (over x).
Axes of the slice: x: 4, y: 8, z: 8, core: 2. Of those that a mesh axis runs over, the one named last changes fastest.
Arguments:
- resid_stream: bfloat16 [384, 8192], P('lat', 'tok'), may hold values from -6 to 6
- enc_weight: bfloat16 [16384, 8192], P('lat', 'tok'), may hold values from -0.0625 to 0.0625
- enc_bias: float32 [16384], P('lat'), may hold values from -3 to 3
- dec_weight: bfloat16 [16384, 8192], P('lat', 'tok'), may hold values from -0.75 to 0.75
- dec_bias: float32 [8192], P('tok'), may hold values from -3 to 3
- active_ids: int32 [384, 64], replicated, may hold values from 0 to 16383, as said below
- active_count: int32 [384], replicated, may hold values from 32 to 64, as said below
Outputs:
- pre_acts: float32 [384, 16384], P(None, 'lat')
- residual: bfloat16 [384, 8192], P('lat', 'tok')
- grad_enc: bfloat16 [16384, 8192], P('lat', 'tok')
- grad_dec: bfloat16 [16384, 8192], P('lat', 'tok')
Inputs may be any that keep to these rules, and one draw needn't show every extreme that they name: `active_ids`: within a row all 64 entries are different latents; entries past the row's count are ordinary latent numbers that are to be ignored; some latent shards are named far more often than others. `active_count`: some row has 64 valid entries and some has 32.
All inputs are finite; a program needn't handle non-finite values.
Results may differ from a plain program's by a relative error of at most 0.0059.
Values may be sent and summed in bfloat16 or wider, within the bound.
A program may use at most 64 MiB of HBM per device.

v0:
```python
import math
import jax
import jax.numpy as jnp
from jax import lax
from jax.sharding import PartitionSpec as P


def active_mask(id_rows, counts, first_latent, latent_count):
    tokens, top_count = id_rows.shape
    block_rows = math.gcd(tokens, 128)
    in_list = jnp.arange(top_count, dtype=jnp.int32)[None, :] < counts[:, None]
    local_ids = jnp.where(in_list, id_rows - first_latent, -1)
    latent_iota = jnp.arange(latent_count, dtype=jnp.int32)

    def one_block(id_block):
        return jnp.any(id_block[:, :, None] == latent_iota[None, None, :], axis=1).astype(
            jnp.float32
        )

    blocks = lax.map(one_block, local_ids.reshape(tokens // block_rows, block_rows, top_count))
    return blocks.reshape(tokens, latent_count)


def shards(resid_stream, enc_weight, enc_bias, dec_weight, dec_bias, active_ids, active_count):
    lat_dev = enc_weight.shape[0]
    rows_own = resid_stream.shape[0]
    full_rows = lax.all_gather(resid_stream, "lat", axis=0, tiled=True)
    partial_value = lax.dot_general(
        full_rows, enc_weight, (((1,), (1,)), ((), ())), preferred_element_type=jnp.float32
    )
    pre_acts = lax.psum(partial_value, "tok") + enc_bias[None, :]
    act_mask = active_mask(active_ids, active_count, lax.axis_index("lat") * lat_dev, lat_dev)
    activations = (pre_acts * act_mask).astype(jnp.bfloat16)
    own_start = lax.axis_index("lat") * rows_own
    rebuilt = lax.psum(jnp.dot(activations, dec_weight, preferred_element_type=jnp.float32), "lat")
    residual_all = (rebuilt + dec_bias[None, :] - full_rows.astype(jnp.float32)).astype(
        jnp.bfloat16
    )
    residual = lax.dynamic_slice_in_dim(residual_all, own_start, rows_own, 0)
    grad_dec = 0.5 * lax.dot_general(
        activations, residual_all, (((0,), (0,)), ((), ())), preferred_element_type=jnp.float32
    )
    back_terms = lax.dot_general(
        residual_all, dec_weight, (((1,), (1,)), ((), ())), preferred_element_type=jnp.float32
    )
    back_terms = lax.psum(back_terms, "tok")
    act_grads = (0.5 * back_terms * act_mask).astype(jnp.bfloat16)
    grad_enc = lax.dot_general(
        act_grads, full_rows, (((0,), (0,)), ((), ())), preferred_element_type=jnp.float32
    )
    return (pre_acts, residual, grad_enc.astype(jnp.bfloat16), grad_dec.astype(jnp.bfloat16))


def solution(mesh):
    placed = (P("lat", "tok"), P("lat", "tok"), P("lat"), P("lat", "tok"), P("tok"), P(), P())
    return jax.shard_map(
        shards,
        mesh=mesh,
        in_specs=placed,
        out_specs=(P(None, "lat"), P("lat", "tok"), P("lat", "tok"), P("lat", "tok")),
        check_vma=False,
    )
```

profile of v0, /device:TPU:8, one launch (start us, length us, event | category | flops | bytes accessed | tf_op | source)
XLA Modules:
  0.0 428.0 jit_solution(15382301777076680504)
XLA Ops:
  7.2 0.0 copy-start
  7.2 0.0 all-gather.3.cloned.1.call-start
  7.2 0.7 all-gather.3.cloned.1.call-update
  7.9 0.0 all-reduce.4.cloned.1.call-start
  8.0 0.9 subtract_select_fusion
  8.9 0.1 copy.14
  9.0 0.0 copy-start.2
  9.0 89.1 %all-gather.3.cloned.1.call-done = bf16[128,3,2048]{2,1,0:T(4,128)(2,1)} async-done(((bf16[1,3,2048]{2,1,0:T(4,128)(2,1)}), bf16[128,3,2048]{2,1,0:T(4,128)(2,1)}) %all-gather.3.cloned.1.call-update) | async-done | bytes 1572880 | tf_op jit(solution)/shard_map/all_gather | solution.py:27
  98.2 3.9 reshape.33
  102.1 0.0 copy-done.2
  102.1 0.0 copy-start.4
  102.1 1.3 fusion.6
  103.4 0.0 all-reduce.4.cloned.1.call-update
  103.4 0.0 all-reduce.6.cloned.1.call-start
  103.4 4.4 %while.11 = (s32[]{:T(128)}, f32[3,128,128]{2,1,0:T(8,128)S(1)}, s32[3,128,64]{2,1,0:T(8,128)S(1)}, s32[]{:T(128)}) while((s32[]{:T(128)}, f32[3,128,128]{2,1,0:T(8,128)S(1)}, s32[3,128,64]{2,1,0:T(8,128)S(1)}, s32[]{:T(128)}) %tuple.37), condition=%wide.region_3.4_spmd.clone, body=%wide.region_1.3_spmd.clone.sunk | while | flops 2097154 | bytes 196677 | solution.py:20
  103.5 1.4 fusion.20
  104.9 1.4 fusion.20
  106.4 1.4 fusion.20
  107.8 45.5 %all-reduce.4.cloned.1.call-done = f32[384,128]{1,0:T(8,128)} async-done(((f32[384,128]{1,0:T(8,128)}), f32[384,128]{1,0:T(8,128)}) %all-reduce.4.cloned.1.call-update) | async-done | bytes 196624 | tf_op jit(solution)/shard_map/psum | solution.py:31
  153.4 0.0 copy-done.4
  153.4 1.6 fusion.4
  155.0 0.0 copy-done
  155.0 2.2 fusion.7
  157.2 0.0 copy-start.3
  157.2 0.0 all-reduce.6.cloned.1.call-update
  157.3 0.0 all-reduce.8.cloned.1.call-start
  157.3 204.0 %all-reduce.6.cloned.1.call-done = f32[384,2048]{1,0:T(8,128)} async-done(((f32[384,2048]{1,0:T(8,128)}), f32[384,2048]{1,0:T(8,128)}) %all-reduce.6.cloned.1.call-update) | async-done | bytes 3145744 | tf_op jit(solution)/shard_map/psum | solution.py:35
  361.3 0.0 copy-done.3
  361.3 2.4 subtract_convert_fusion
  363.8 0.0 copy-start.1
  363.8 1.1 copy-done.1
  364.9 1.3 fusion.8
  366.2 2.7 fusion.3
  368.9 0.0 all-reduce.8.cloned.1.call-update
  368.9 1.5 constant_dynamic-slice_fusion
  370.4 48.8 %all-reduce.8.cloned.1.call-done = f32[384,128]{1,0:T(8,128)} async-done(((f32[384,128]{1,0:T(8,128)}), f32[384,128]{1,0:T(8,128)}) %all-reduce.8.cloned.1.call-update) | async-done | bytes 196624 | tf_op jit(solution)/shard_map/psum | solution.py:46
  419.2 1.0 fusion.5
  420.2 1.3 convolution_convert_fusion
  (7 shorter events, 0.1 us)
Async XLA Ops:
  7.2 147.8 %copy-start = (bf16[128,2048]{1,0:T(8,128)(2,1)S(1)}, bf16[128,2048]{1,0:T(8,128)(2,1)}, u32[]{:S(2)}) copy-start(bf16[128,2048]{1,0:T(8,128)(2,1)} %param.12) | copy-start | bytes 1572868
  7.2 91.0 %all-gather.3.cloned.1.call-start = ((), (), s32[]{:S(2)}) async-start(), calls=%async_computation.3 | async-start | bytes 2113536 | tf_op jit(solution)/shard_map/all_gather | solution.py:27
  7.9 145.4 %all-reduce.4.cloned.1.call-start = ((), (), s32[]{:S(2)}) async-start(), calls=%async_computation | async-start | bytes 393216 | tf_op jit(solution)/shard_map/psum | solution.py:31
  9.0 93.1 %copy-start.2 = (bf16[128,2048]{1,0:T(8,128)(2,1)S(1)}, bf16[128,2048]{1,0:T(8,128)(2,1)}, u32[]{:S(2)}) copy-start(bf16[128,2048]{1,0:T(8,128)(2,1)} %param.10) | copy-start | bytes 1572868
  102.1 51.3 %copy-start.4 = (f32[128]{0:T(128)S(1)}, f32[128]{0:T(128)}, u32[]{:S(2)}) copy-start(f32[128]{0:T(128)} %param.11) | copy-start | bytes 1540
  103.4 257.9 %all-reduce.6.cloned.1.call-start = ((), (), s32[]{:S(2)}) async-start(), calls=%async_computation.1 | async-start | bytes 6291456 | tf_op jit(solution)/shard_map/psum | solution.py:35
  157.2 204.1 %copy-start.3 = (f32[2048]{0:T(1024)S(1)}, f32[2048]{0:T(1024)}, u32[]{:S(2)}) copy-start(f32[2048]{0:T(1024)} %param.13) | copy-start | bytes 24580
  157.3 262.0 %all-reduce.8.cloned.1.call-start = ((), (), s32[]{:S(2)}) async-start(), calls=%async_computation.2 | async-start | bytes 393216 | tf_op jit(solution)/shard_map/psum | solution.py:46
  363.8 1.1 copy-start.1
Sparse Core Ops, SparseCore 0:
  11.1 87.0 all-gather.2
  103.5 49.7 all-reduce.3
  157.4 203.9 all-reduce.5
  369.0 50.1 all-reduce.7
where the time goes:
time: 428 us
  waiting for transfers between devices  388 us (91%)
  between operations  13.9 us (3%)
  other arithmetic  10.2 us (2%)
  matrix products  8.72 us (2%)
  local copies, waits for them, and re-layouts  6.7 us (2%)
    psum x1, waiting for transfers between devices, shards(): lax.psum(jnp.dot(activations, dec_weight, preferred_element_type=jnp.floa...  204 us
    all_gather x1, waiting for transfers between devices, shards(): full_rows = lax.all_gather(resid_stream, 'lat', axis=0, tiled=True)  89.1 us
    psum x1, waiting for transfers between devices, shards(): back_terms = lax.psum(back_terms, 'tok')  48.8 us
    psum x1, waiting for transfers between devices, shards(): pre_acts = lax.psum(partial_value, 'tok') + enc_bias[None, :]  45.5 us
  transfers between devices with their start and end apart: 4, of which 4 were waited for; matrix products, arithmetic and copies ran while one was open for 2% of the time, Pallas kernels for 0%

commit v1 on v0

--- a/solution.py
+++ b/solution.py
@@ -24,7 +24,9 @@
 def shards(resid_stream, enc_weight, enc_bias, dec_weight, dec_bias, active_ids, active_count):
     lat_dev = enc_weight.shape[0]
     rows_own = resid_stream.shape[0]
-    full_rows = lax.all_gather(resid_stream, "lat", axis=0, tiled=True)
+    full_rows = jnp.concatenate(
+        lax.all_to_all(jnp.stack([resid_stream] * lax.axis_size("lat")), "lat", 0, 0), axis=0
+    )
     partial_value = lax.dot_general(
         full_rows, enc_weight, (((1,), (1,)), ((), ())), preferred_element_type=jnp.float32
     )

time: 428 us -> 408 us (0.953)
  waiting for transfers between devices: 388 us -> 348 us
  starting transfers between devices: 0.16 us -> 18.1 us
    all_gather x1 -> x0, waiting for transfers between devices: 89.1 us -> none  [shards(): full_rows = lax.all_gather(resid_stream, 'lat', axis=0, tiled=True)]
    all_to_all x0 -> x1, waiting for transfers between devices: none -> 53.4 us  [shards(): lax.all_to_all(jnp.stack([resid_stream] * lax.axis_size('lat')), 'lat', 0...]
    all_to_all x0 -> x1, starting transfers between devices: none -> 18 us  [shards(): lax.all_to_all(jnp.stack([resid_stream] * lax.axis_size('lat')), 'lat', 0...]
  transfers between devices with their start and end apart: 4 -> 4, of which waited for: 4 -> 4; matrix products, arithmetic and copies ran while one was open for 2% -> 1% of each run, Pallas kernels for 0% -> 0%
where the time goes in v1:
time: 408 us; the launch traced here: 407 us
  waiting for transfers between devices  348 us (85%)
  starting transfers between devices  18.1 us (4%)
  between operations  13.9 us (3%)
  local copies, waits for them, and re-layouts  9.84 us (2%)
  other arithmetic  9.24 us (2%)
  matrix products  8.73 us (2%)
    psum x1, waiting for transfers between devices, shards(): lax.psum(jnp.dot(activations, dec_weight, preferred_element_type=jnp.floa...  204 us
    all_to_all x1, waiting for transfers between devices, shards(): lax.all_to_all(jnp.stack([resid_stream] * lax.axis_size('lat')), 'lat', 0...  53.4 us
    psum x1, waiting for transfers between devices, shards(): back_terms = lax.psum(back_terms, 'tok')  48.9 us
    psum x1, waiting for transfers between devices, shards(): pre_acts = lax.psum(partial_value, 'tok') + enc_bias[None, :]  41.3 us
    all_to_all x1, starting transfers between devices, shards(): lax.all_to_all(jnp.stack([resid_stream] * lax.axis_size('lat')), 'lat', 0...  18 us
  transfers between devices with their start and end apart: 4, of which 4 were waited for; matrix products, arithmetic and copies ran while one was open for 1% of the time, Pallas kernels for 0%

profile of v1, /device:TPU:8, one launch (start us, length us, event | category | flops | bytes accessed | tf_op | source)
XLA Modules:
  0.0 407.5 jit_solution(828840086550292007)
XLA Ops:
  7.2 0.0 copy-start
  7.2 3.1 stack.2
  10.3 0.0 copy-start.3
  10.3 0.0 copy-start.5
  10.3 18.0 %all-to-all-start = ((bf16[128,3,2048]{2,1,0:T(4,128)(2,1)}), bf16[128,3,2048]{2,1,0:T(4,128)(2,1)}, u32[]{:S(2)}, u32[]{:S(2)}) async-start(bf16[128,3,2048]{2,1,0:T(4,128)(2,1)} %stack.2), calls=%async_computation | async-start | bytes 4194304 | tf_op jit(solution)/shard_map/all_to_all | solution.py:28
  28.3 0.0 all-reduce.4.cloned.1.call-start
  28.3 0.0 copy-done.3
  28.4 0.0 copy-done.5
  28.4 0.1 copy.13
  28.5 0.0 copy-start.2
  28.5 53.4 %all-to-all-done = bf16[128,3,2048]{2,1,0:T(4,128)(2,1)} async-done(((bf16[128,3,2048]{2,1,0:T(4,128)(2,1)}), bf16[128,3,2048]{2,1,0:T(4,128)(2,1)}, u32[]{:S(2)}, u32[]{:S(2)}) %all-to-all-start) | async-done | bytes 1572896 | tf_op jit(solution)/shard_map/all_to_all | solution.py:28
  81.9 3.9 reshape.34
  85.9 0.0 copy-done.2
  85.9 0.0 copy-start.6
  85.9 1.3 fusion.6
  87.1 0.0 all-reduce.4.cloned.1.call-update
  87.2 0.0 all-reduce.6.cloned.1.call-start
  87.2 4.4 %while.11 = (s32[]{:T(128)}, f32[3,128,128]{2,1,0:T(8,128)S(1)}, s32[3,128,64]{2,1,0:T(8,128)S(1)}, s32[]{:T(128)}) while((s32[]{:T(128)}, f32[3,128,128]{2,1,0:T(8,128)S(1)}, s32[3,128,64]{2,1,0:T(8,128)S(1)}, s32[]{:T(128)}) %tuple.35), condition=%wide.region_3.4_spmd.clone, body=%wide.region_1.3_spmd.clone.sunk | while | flops 2097154 | bytes 196677 | solution.py:20
  87.2 1.4 fusion.20
  88.7 1.4 fusion.20
  90.2 1.4 fusion.20
  91.6 41.3 %all-reduce.4.cloned.1.call-done = f32[384,128]{1,0:T(8,128)} async-done(((f32[384,128]{1,0:T(8,128)}), f32[384,128]{1,0:T(8,128)}) %all-reduce.4.cloned.1.call-update) | async-done | bytes 196624 | tf_op jit(solution)/shard_map/psum | solution.py:33
  132.9 0.0 copy-done.6
  132.9 1.6 fusion.4
  134.5 0.0 copy-done
  134.5 2.3 fusion.7
  136.8 0.0 copy-start.4
  136.8 0.0 all-reduce.6.cloned.1.call-update
  136.8 0.0 all-reduce.8.cloned.1.call-start
  136.9 204.0 %all-reduce.6.cloned.1.call-done = f32[384,2048]{1,0:T(8,128)} async-done(((f32[384,2048]{1,0:T(8,128)}), f32[384,2048]{1,0:T(8,128)}) %all-reduce.6.cloned.1.call-update) | async-done | bytes 3145744 | tf_op jit(solution)/shard_map/psum | solution.py:37
  340.9 0.0 copy-done.4
  340.9 2.4 subtract_convert_fusion
  343.3 0.0 copy-start.1
  343.3 1.1 copy-done.1
  344.4 1.3 fusion.8
  345.7 2.7 fusion.3
  348.4 0.0 all-reduce.8.cloned.1.call-update
  348.4 1.5 constant_dynamic-slice_fusion
  349.9 48.9 %all-reduce.8.cloned.1.call-done = f32[384,128]{1,0:T(8,128)} async-done(((f32[384,128]{1,0:T(8,128)}), f32[384,128]{1,0:T(8,128)}) %all-reduce.8.cloned.1.call-update) | async-done | bytes 196624 | tf_op jit(solution)/shard_map/psum | solution.py:48
  398.7 1.0 fusion.5
  399.7 1.3 convolution_convert_fusion
  (8 shorter events, 0.1 us)
Async XLA Ops:
  7.2 127.4 %copy-start = (bf16[128,2048]{1,0:T(8,128)(2,1)S(1)}, bf16[128,2048]{1,0:T(8,128)(2,1)}, u32[]{:S(2)}) copy-start(bf16[128,2048]{1,0:T(8,128)(2,1)} %param.12) | copy-start | bytes 1572868
  10.3 18.0 %copy-start.3 = (s32[384,64]{0,1:T(8,128)S(1)}, s32[384,64]{0,1:T(8,128)}, u32[]{:S(2)}) copy-start(s32[384,64]{0,1:T(8,128)} %param.14) | copy-start | bytes 294916
  10.3 18.0 %copy-start.5 = (s32[384]{0:T(512)S(1)}, s32[384]{0:T(512)}, u32[]{:S(2)}) copy-start(s32[384]{0:T(512)} %param.15) | copy-start | bytes 4612
  10.3 71.6 %all-to-all-start = ((bf16[128,3,2048]{2,1,0:T(4,128)(2,1)}), bf16[128,3,2048]{2,1,0:T(4,128)(2,1)}, u32[]{:S(2)}, u32[]{:S(2)}) async-start(bf16[128,3,2048]{2,1,0:T(4,128)(2,1)} %stack.2), calls=%async_computation | async-start | bytes 4194304 | tf_op jit(solution)/shard_map/all_to_all | solution.py:28
  28.3 104.6 %all-reduce.4.cloned.1.call-start = ((), (), s32[]{:S(2)}) async-start(), calls=%async_computation.1 | async-start | bytes 393216 | tf_op jit(solution)/shard_map/psum | solution.py:33
  28.5 57.3 %copy-start.2 = (bf16[128,2048]{1,0:T(8,128)(2,1)S(1)}, bf16[128,2048]{1,0:T(8,128)(2,1)}, u32[]{:S(2)}) copy-start(bf16[128,2048]{1,0:T(8,128)(2,1)} %param.10) | copy-start | bytes 1572868
  85.9 47.0 %copy-start.6 = (f32[128]{0:T(128)S(1)}, f32[128]{0:T(128)}, u32[]{:S(2)}) copy-start(f32[128]{0:T(128)} %param.11) | copy-start | bytes 1540
  87.2 253.7 %all-reduce.6.cloned.1.call-start = ((), (), s32[]{:S(2)}) async-start(), calls=%async_computation.2 | async-start | bytes 6291456 | tf_op jit(solution)/shard_map/psum | solution.py:37
  136.8 204.1 %copy-start.4 = (f32[2048]{0:T(1024)S(1)}, f32[2048]{0:T(1024)}, u32[]{:S(2)}) copy-start(f32[2048]{0:T(1024)} %param.13) | copy-start | bytes 24580
  136.8 261.9 %all-reduce.8.cloned.1.call-start = ((), (), s32[]{:S(2)}) async-start(), calls=%async_computation.3 | async-start | bytes 393216 | tf_op jit(solution)/shard_map/psum | solution.py:48
  343.3 1.1 copy-start.1
Sparse Core Ops, SparseCore 0:
  87.3 45.5 all-reduce.3
  136.9 203.9 all-reduce.5
  348.5 50.1 all-reduce.7

commit v2 on v0

--- a/solution.py
+++ b/solution.py
@@ -28,7 +28,7 @@
     partial_value = lax.dot_general(
         full_rows, enc_weight, (((1,), (1,)), ((), ())), preferred_element_type=jnp.float32
     )
-    pre_acts = lax.psum(partial_value, "tok") + enc_bias[None, :]
+    pre_acts = jnp.sum(lax.all_gather(partial_value, "tok"), axis=0) + enc_bias[None, :]
     act_mask = active_mask(active_ids, active_count, lax.axis_index("lat") * lat_dev, lat_dev)
     activations = (pre_acts * act_mask).astype(jnp.bfloat16)
     own_start = lax.axis_index("lat") * rows_own

time: 428 us -> 388 us (0.907)
  waiting for transfers between devices: 388 us -> 335 us
  blocking collectives: 0 us -> 13.9 us
    psum x1 -> x0, waiting for transfers between devices: 45.5 us -> none  [shards(): pre_acts = lax.psum(partial_value, 'tok') + enc_bias[None, :]]
    all_gather x0 -> x1, blocking collectives: none -> 13.9 us  [shards(): lax.all_gather(partial_value, 'tok')]
    all_gather x1, waiting for transfers between devices: 89.1 us -> 84.7 us  [shards(): full_rows = lax.all_gather(resid_stream, 'lat', axis=0, tiled=True)]
  transfers between devices with their start and end apart: 4 -> 3, of which waited for: 4 -> 3; matrix products, arithmetic and copies ran while one was open for 2% -> 2% of each run, Pallas kernels for 0% -> 0%
where the time goes in v2:
time: 388 us; the launch traced here: 387 us
  waiting for transfers between devices  335 us (86%)
  blocking collectives  13.9 us (4%)
  between operations  13.9 us (4%)
  other arithmetic  9.25 us (2%)
  matrix products  8.03 us (2%)
  local copies, waits for them, and re-layouts  6.72 us (2%)
    psum x1, waiting for transfers between devices, shards(): lax.psum(jnp.dot(activations, dec_weight, preferred_element_type=jnp.floa...  201 us
    all_gather x1, waiting for transfers between devices, shards(): full_rows = lax.all_gather(resid_stream, 'lat', axis=0, tiled=True)  84.7 us
    psum x1, waiting for transfers between devices, shards(): back_terms = lax.psum(back_terms, 'tok')  48.9 us
    all_gather x1, blocking collectives, shards(): lax.all_gather(partial_value, 'tok')  13.9 us
  transfers between devices with their start and end apart: 3, of which 3 were waited for; matrix products, arithmetic and copies ran while one was open for 2% of the time, Pallas kernels for 0%

profile of v2, /device:TPU:8, one launch (start us, length us, event | category | flops | bytes accessed | tf_op | source)
XLA Modules:
  0.0 387.3 jit_solution(8300959401381647880)
XLA Ops:
  7.2 0.0 copy-start
  7.2 0.0 all-gather.4.cloned.1.call-start
  7.2 0.7 all-gather.4.cloned.1.call-update
  7.9 0.0 all-reduce.3.cloned.1.call-start
  8.0 0.9 subtract_select_fusion
  8.9 0.1 copy.14
  9.0 4.4 %while.11 = (s32[]{:T(128)}, f32[3,128,128]{2,1,0:T(8,128)S(1)}, s32[3,128,64]{2,1,0:T(8,128)S(1)}, s32[]{:T(128)}) while((s32[]{:T(128)}, f32[3,128,128]{2,1,0:T(8,128)S(1)}, s32[3,128,64]{2,1,0:T(8,128)S(1)}, s32[]{:T(128)}) %tuple.35), condition=%wide.region_3.4_spmd.clone, body=%wide.region_1.3_spmd.clone.sunk | while | flops 2097154 | bytes 196677 | solution.py:20
  9.1 1.4 fusion.20
  10.5 1.4 fusion.20
  12.0 1.4 fusion.20
  13.4 0.0 copy-start.2
  13.4 84.7 %all-gather.4.cloned.1.call-done = bf16[128,3,2048]{2,1,0:T(4,128)(2,1)} async-done(((bf16[1,3,2048]{2,1,0:T(4,128)(2,1)}), bf16[128,3,2048]{2,1,0:T(4,128)(2,1)}) %all-gather.4.cloned.1.call-update) | async-done | bytes 1572880 | tf_op jit(solution)/shard_map/all_gather | solution.py:27
  98.2 3.9 %reshape.34 = bf16[384,2048]{1,0:T(8,128)(2,1)S(1)} reshape(bf16[128,3,2048]{2,1,0:T(4,128)(2,1)} %all-gather.4.cloned.1.call-done) | data formatting | bytes 3145728
  102.1 0.0 copy-done.2
  102.1 0.0 copy-start.4
  102.1 0.6 fusion.6
  102.7 13.9 %all-gather = f32[1536,128]{1,0:T(8,128)S(1)} all-gather(f32[384,128]{1,0:T(8,128)S(1)} %fusion.6), channel_id=2, replica_groups=mesh['lat'=128,'tok'=4] {'tok'}, dimensions={0}, use_global_device_ids=true | all-gather | bytes 983040 | tf_op jit(solution)/shard_map/all_gather | solution.py:31
  116.7 0.0 copy-done.4
  116.7 0.7 fusion.4
  117.4 0.0 copy-done
  117.4 2.2 fusion.7
  119.6 0.0 copy-start.3
  119.6 0.0 all-reduce.3.cloned.1.call-update
  119.6 0.0 all-reduce.5.cloned.1.call-start
  119.7 201.0 %all-reduce.3.cloned.1.call-done = f32[384,2048]{1,0:T(8,128)} async-done(((f32[384,2048]{1,0:T(8,128)}), f32[384,2048]{1,0:T(8,128)}) %all-reduce.3.cloned.1.call-update) | async-done | bytes 3145744 | tf_op jit(solution)/shard_map/psum | solution.py:35
  320.7 0.0 copy-done.3
  320.7 2.4 subtract_convert_fusion
  323.1 0.0 copy-start.1
  323.1 1.2 copy-done.1
  324.2 1.3 fusion.8
  325.5 2.7 fusion.3
  328.2 0.0 all-reduce.5.cloned.1.call-update
  328.2 1.5 constant_dynamic-slice_fusion
  329.7 48.9 %all-reduce.5.cloned.1.call-done = f32[384,128]{1,0:T(8,128)} async-done(((f32[384,128]{1,0:T(8,128)}), f32[384,128]{1,0:T(8,128)}) %all-reduce.5.cloned.1.call-update) | async-done | bytes 196624 | tf_op jit(solution)/shard_map/psum | solution.py:46
  378.6 1.0 fusion.5
  379.5 1.3 convolution_convert_fusion
  (8 shorter events, 0.1 us)
Async XLA Ops:
  7.2 110.2 %copy-start = (bf16[128,2048]{1,0:T(8,128)(2,1)S(1)}, bf16[128,2048]{1,0:T(8,128)(2,1)}, u32[]{:S(2)}) copy-start(bf16[128,2048]{1,0:T(8,128)(2,1)} %param.12) | copy-start | bytes 1572868
  7.2 91.0 %all-gather.4.cloned.1.call-start = ((), (), s32[]{:S(2)}) async-start(), calls=%async_computation.2 | async-start | bytes 2113536 | tf_op jit(solution)/shard_map/all_gather | solution.py:27
  7.9 312.8 %all-reduce.3.cloned.1.call-start = ((), (), s32[]{:S(2)}) async-start(), calls=%async_computation | async-start | bytes 6291456 | tf_op jit(solution)/shard_map/psum | solution.py:35
  13.4 88.7 %copy-start.2 = (bf16[128,2048]{1,0:T(8,128)(2,1)S(1)}, bf16[128,2048]{1,0:T(8,128)(2,1)}, u32[]{:S(2)}) copy-start(bf16[128,2048]{1,0:T(8,128)(2,1)} %param.10) | copy-start | bytes 1572868
  102.1 14.6 %copy-start.4 = (f32[128]{0:T(128)S(1)}, f32[128]{0:T(128)}, u32[]{:S(2)}) copy-start(f32[128]{0:T(128)} %param.11) | copy-start | bytes 1540
  119.6 201.1 %copy-start.3 = (f32[2048]{0:T(1024)S(1)}, f32[2048]{0:T(1024)}, u32[]{:S(2)}) copy-start(f32[2048]{0:T(1024)} %param.13) | copy-start | bytes 24580
  119.6 258.9 %all-reduce.5.cloned.1.call-start = ((), (), s32[]{:S(2)}) async-start(), calls=%async_computation.1 | async-start | bytes 393216 | tf_op jit(solution)/shard_map/psum | solution.py:46
  323.1 1.2 copy-start.1
Sparse Core Ops, SparseCore 0:
  11.1 87.0 all-gather.3
  119.8 200.8 all-reduce.2
  328.4 50.1 all-reduce.4
